TPU v7x, 512 devices: a whole 4x8x8 slice. The times are simulated.
512 devices in a mesh: band: 64 (over z, x, core), mem: 8 (over y).
Axes of the slice: x: 4, y: 8, z: 8, core: 2. Of those that a mesh axis runs over, the one named last changes fastest.
Arguments:
- spectra: bfloat16 [16, 4, 2, 2, 901120], P('mem', None, None, None, 'band'), may hold values from -6 to 6
- legendre: bfloat16 [40, 901120], P(None, 'band'), may hold values from -0.0034179688 to 0.0034179688
- pair_waves: int32 [640], P('band'), may hold values from 0 to 639, each once
- band_lengths: int32 [64], replicated, may hold values from 1 to 2, 80 in all
- eof_basis: bfloat16 [128, 2560, 256], P('band'), may hold values from -0.0390625 to 0.0390625
Outputs:
- grid_fields: bfloat16 [16, 4, 2, 128, 2560], P('mem', None, None, 'band')
- eof_coeffs: float32 [16, 4, 2, 256], P('mem', None, None, 'band')
Inputs may be any that keep to these rules, and one draw needn't show every extreme that they name: `pair_waves`: every lower wavenumber 0 .. 639 stands in exactly one pair slot. `band_lengths`: the lengths sum to 80; some band has exactly 2 rows.
All inputs are finite; a program needn't handle non-finite values.
Results may differ from a plain program's by a relative error of at most 0.0055.
Values may be sent and summed in bfloat16 or wider, within the bound.
No kernel may reach another device: no remote copies, remote signals or barrier semaphores. Data moves between devices by JAX's collectives and lax.ppermute only.
A program may use at most 192 MiB of HBM per device.

v0:
```python
import math
import jax
import jax.numpy as jnp
from jax import lax
from jax.sharding import PartitionSpec as P

WAVE_COUNT = 1280
BLK = 128


def wave_block(orders, start, width, length):
    lon_index = start + jnp.arange(width, dtype=jnp.int32)
    phase_idx = orders[..., None] * lon_index % length
    angle_rad = phase_idx.astype(jnp.float32) * (2.0 * math.pi / length)
    weight = jnp.where(orders == 0, 1.0, 2.0).astype(jnp.float32)[..., None]
    return jnp.stack([weight * jnp.cos(angle_rad), -weight * jnp.sin(angle_rad)]).astype(
        jnp.bfloat16
    )


def shards(spectra, legendre, pair_waves, band_lengths, eof_basis):
    ens_dev, fields, level_stack, re_im, slot_count = spectra.shape
    lat_half = legendre.shape[0]
    pairs_dev = pair_waves.shape[0]
    blocks = slot_count // (pairs_dev * BLK)
    columns = ens_dev * fields * level_stack * re_im
    band_count = lax.axis_size("band")
    most_rows, longitudes, eof_modes = eof_basis.shape
    spectral_data = spectra.reshape(columns, pairs_dev, blocks, BLK)
    legendre_rows = legendre.reshape(lat_half, pairs_dev, blocks, BLK)
    position = jnp.arange(blocks * BLK, dtype=jnp.int32).reshape(1, blocks, BLK)
    lower_wave = pair_waves.reshape(pairs_dev, 1, 1)
    low_blocks = WAVE_COUNT // BLK - lower_wave // BLK
    upper_pos = position - low_blocks * BLK
    in_range = (position < WAVE_COUNT - lower_wave) | (upper_pos >= 0) & (
        upper_pos < lower_wave + 1
    )
    spectral_data = spectral_data * in_range.astype(jnp.bfloat16)[None]
    block_index = jnp.arange(blocks, dtype=jnp.int32)[None, :]
    low_owner = (block_index < low_blocks[:, :, 0]).astype(jnp.float32)
    owners = jnp.stack([low_owner, 1.0 - low_owner], axis=1)
    alternate = jnp.where(jnp.arange(BLK) % 2 == 0, 1.0, -1.0).astype(jnp.bfloat16)
    north_part = jnp.einsum(
        "cptk,jptk->ptcj", spectral_data, legendre_rows, preferred_element_type=jnp.float32
    )
    south_part = jnp.einsum(
        "cptk,jptk->ptcj",
        spectral_data,
        legendre_rows * alternate,
        preferred_element_type=jnp.float32,
    )
    rows_all = jnp.concatenate([north_part, south_part[..., ::-1]], axis=-1)
    fourier = jnp.einsum(
        "pht,ptcj->jphc", owners, rows_all, precision=lax.Precision.HIGHEST
    ).astype(jnp.bfloat16)
    starts = jnp.cumsum(band_lengths) - band_lengths
    offsets = jnp.arange(most_rows, dtype=jnp.int32)
    row_index = jnp.minimum(starts[:, None] + offsets[None, :], 2 * lat_half - 1).reshape(-1)
    packed = jnp.take(fourier, row_index, axis=0).reshape(
        band_count, most_rows, pairs_dev * 2 * columns
    )
    arrived = lax.all_to_all(packed, "band", split_axis=0, concat_axis=0, tiled=True)
    all_waves = lax.all_gather(pair_waves, "band", axis=0, tiled=True).reshape(
        band_count, pairs_dev
    )
    lower_all = all_waves.T
    orders = jnp.stack([lower_all, WAVE_COUNT - 1 - lower_all], axis=1)
    arrived = arrived.reshape(
        band_count, most_rows, pairs_dev, 2, ens_dev, fields, level_stack, re_im
    )
    lon_width = math.gcd(longitudes, 512)
    lon_blocks = longitudes // lon_width

    def synth_block(block_number):
        table_part = wave_block(orders, block_number * lon_width, lon_width, longitudes)
        return jnp.einsum(
            "srphabdc,cphsk->abdrk", arrived, table_part, preferred_element_type=jnp.float32
        )

    grid_parts = lax.map(synth_block, jnp.arange(lon_blocks, dtype=jnp.int32))
    grid_sum = jnp.moveaxis(grid_parts, 0, 4).reshape(
        ens_dev, fields, level_stack, most_rows, longitudes
    )
    own_rows = band_lengths[lax.axis_index("band")]
    row_keep = (offsets < own_rows).astype(jnp.float32)
    grid_fields = (grid_sum * row_keep[:, None]).astype(jnp.bfloat16)
    flat_grid = grid_fields.reshape(ens_dev * fields * level_stack, most_rows * longitudes)
    partial_value = jnp.dot(
        flat_grid,
        eof_basis.reshape(most_rows * longitudes, eof_modes),
        preferred_element_type=jnp.float32,
    )
    share_width = eof_modes // band_count
    summed_all = lax.psum(partial_value, "band")
    own_share = lax.dynamic_slice_in_dim(
        summed_all, lax.axis_index("band") * share_width, share_width, 1
    )
    local_share = own_share.reshape(ens_dev, fields * level_stack, share_width)
    summed = lax.psum(jnp.sum(local_share, axis=0), "mem")
    anomaly = local_share - summed / (ens_dev * lax.axis_size("mem"))
    return (grid_fields, anomaly.reshape(ens_dev, fields, level_stack, share_width))


def solution(mesh):
    return jax.shard_map(
        shards,
        mesh=mesh,
        in_specs=(
            P("mem", None, None, None, "band"),
            P(None, "band"),
            P("band"),
            P(),
            P("band", None, None),
        ),
        out_specs=(P("mem", None, None, "band", None), P("mem", None, None, "band")),
        check_vma=False,
    )
```

profile of v0, /device:TPU:8, one launch (start us, length us, event | category | flops | bytes accessed | tf_op | source)
XLA Modules:
  0.0 406.1 jit_solution(17721014867123769294)
XLA Ops:
  0.7 0.8 broadcast_subtract_fusion.2
  1.5 0.1 broadcast_subtract_fusion.1
  1.6 0.1 compare_convert_fusion
  1.7 0.7 copy.36
  2.4 0.1 reduce-window.9
  2.5 0.1 reduce
  2.6 0.7 sub.62
  3.3 2.6 reshape.297
  5.9 3.4 reshape.301
  9.3 0.1 fusion.26
  9.4 1.5 broadcast_multiply_fusion.1
  10.9 0.2 copy-done.1
  11.1 0.1 broadcast_multiply_fusion
  11.2 2.0 fusion.20
  13.2 2.0 fusion.18
  15.2 4.0 rev.3
  19.2 2.6 pad_maximum_fusion
  21.8 3.3 fusion.15
  25.1 0.4 copy.44
  25.5 0.1 copy.43
  25.6 0.1 min.22
  25.8 2.7 gather_fusion
  28.5 1.8 gather.7
  30.2 0.1 copy.37
  30.4 0.9 broadcast_select_fusion
  31.3 13.8 %all-to-all-start = ((bf16[64,2,640]{2,1,0:T(2,128)(2,1)}), bf16[64,2,640]{2,1,0:T(2,128)(2,1)S(1)}, u32[]{:S(2)}, u32[]{:S(2)}) async-start(bf16[64,2,640]{2,1,0:T(2,128)(2,1)} %broadcast_select_fusion), calls=%async_computation | async-start | bytes 327680 | tf_op jit(solution)/shard_map/all_to_all | solution.py:62
  45.1 1.3 dynamic-slice
  47.1 0.2 dynamic-update-slice
  47.4 20.9 %all-reduce = s32[640]{0:T(1024)S(1)} all-reduce(s32[640]{0:T(1024)S(1)} %dynamic-update-slice), channel_id=1, replica_groups=mesh['band'=64,'mem'=8] {'band'}, use_global_device_ids=true, to_apply=%add | all-reduce | flops 640 | bytes 5120
  68.3 0.1 reshape.294
  68.4 0.1 copy.35
  68.6 0.7 dynamic_slice.13
  69.3 0.7 compare_convert_fusion.1
  70.0 0.3 copy.45
  70.3 0.8 copy.47
  71.1 68.8 %while.12 = (s32[]{:T(128)}, f32[5,2,4,2,2,512]{5,2,3,1,4,0:T(4,128)S(1)}, s32[10,2,64]{2,0,1:T(8,128)S(1)}, s32[5]{0:T(128)S(1)}, bf16[64,2,10,2,2,4,2,2]{0,5,2,3,7,6,4,1:T(4,128)(2,1)}, /*index=5*/s32[]{:T(128)}, s32[1]{0:T(128)}) while((s32[]{:T(128)}, f32[5,2,4,2,2,512]{5,2,3,1,4,0:T(4,128)S(1)}, s32[10,2,64]{2,0,1:T(8,128)S(1)}, ...), condition=%wide.region_2.3_spmd, body=%wide.region_1.2_spmd.sunk | while | flops 97652992 | bytes 6326409 | solution.py:80
  71.1 0.6 dynamic_slice.17
  72.4 11.9 %multiply_convert_fusion.5 = (bf16[1,10,2,64,512]{4,3,1,2,0:T(8,128)(2,1)S(1)}, bf16[1,10,2,64,512]{4,3,1,2,0:T(8,128)(2,1)S(1)}) fusion(s32[512]{0:T(512)S(1)} %iota_add_fusion.2, s32[10,2,64]{2,0,1:T(8,128)S(1)} %get-tuple-element.159, f32[10,2,64]{2,0,1:T(8,128)S(1)} %get-tuple-element.139, f32[10,2,64]{2,0,1:T(8,128)S(1)} %get-tuple-element.140), kind=kLoop, calls=%fused_computation.6.clone.1 | loop fusion | flops 8519680 | bytes 2638848 | tf_op jit(solution)/shard_map/convert
  84.3 0.6 fusion.42
  84.9 0.6 dynamic_slice.17
  86.1 11.9 %multiply_convert_fusion.5 = (bf16[1,10,2,64,512]{4,3,1,2,0:T(8,128)(2,1)S(1)}, bf16[1,10,2,64,512]{4,3,1,2,0:T(8,128)(2,1)S(1)}) fusion(s32[512]{0:T(512)S(1)} %iota_add_fusion.2, s32[10,2,64]{2,0,1:T(8,128)S(1)} %get-tuple-element.159, f32[10,2,64]{2,0,1:T(8,128)S(1)} %get-tuple-element.139, f32[10,2,64]{2,0,1:T(8,128)S(1)} %get-tuple-element.140), kind=kLoop, calls=%fused_computation.6.clone.1 | loop fusion | flops 8519680 | bytes 2638848 | tf_op jit(solution)/shard_map/convert
  98.0 0.6 fusion.42
  98.6 0.6 dynamic_slice.17
  99.9 11.9 %multiply_convert_fusion.5 = (bf16[1,10,2,64,512]{4,3,1,2,0:T(8,128)(2,1)S(1)}, bf16[1,10,2,64,512]{4,3,1,2,0:T(8,128)(2,1)S(1)}) fusion(s32[512]{0:T(512)S(1)} %iota_add_fusion.2, s32[10,2,64]{2,0,1:T(8,128)S(1)} %get-tuple-element.159, f32[10,2,64]{2,0,1:T(8,128)S(1)} %get-tuple-element.139, f32[10,2,64]{2,0,1:T(8,128)S(1)} %get-tuple-element.140), kind=kLoop, calls=%fused_computation.6.clone.1 | loop fusion | flops 8519680 | bytes 2638848 | tf_op jit(solution)/shard_map/convert
  111.8 0.6 fusion.42
  112.4 0.6 dynamic_slice.17
  113.7 11.9 %multiply_convert_fusion.5 = (bf16[1,10,2,64,512]{4,3,1,2,0:T(8,128)(2,1)S(1)}, bf16[1,10,2,64,512]{4,3,1,2,0:T(8,128)(2,1)S(1)}) fusion(s32[512]{0:T(512)S(1)} %iota_add_fusion.2, s32[10,2,64]{2,0,1:T(8,128)S(1)} %get-tuple-element.159, f32[10,2,64]{2,0,1:T(8,128)S(1)} %get-tuple-element.139, f32[10,2,64]{2,0,1:T(8,128)S(1)} %get-tuple-element.140), kind=kLoop, calls=%fused_computation.6.clone.1 | loop fusion | flops 8519680 | bytes 2638848 | tf_op jit(solution)/shard_map/convert
  125.6 0.6 fusion.42
  126.2 0.6 dynamic_slice.17
  127.4 11.9 %multiply_convert_fusion.5 = (bf16[1,10,2,64,512]{4,3,1,2,0:T(8,128)(2,1)S(1)}, bf16[1,10,2,64,512]{4,3,1,2,0:T(8,128)(2,1)S(1)}) fusion(s32[512]{0:T(512)S(1)} %iota_add_fusion.2, s32[10,2,64]{2,0,1:T(8,128)S(1)} %get-tuple-element.159, f32[10,2,64]{2,0,1:T(8,128)S(1)} %get-tuple-element.139, f32[10,2,64]{2,0,1:T(8,128)S(1)} %get-tuple-element.140), kind=kLoop, calls=%fused_computation.6.clone.1 | loop fusion | flops 8519680 | bytes 2638848 | tf_op jit(solution)/shard_map/convert
  139.3 0.6 fusion.42
  139.9 0.1 multiply_convert_fusion.2
  140.1 0.1 copy.49
  140.2 0.2 convert_element_type.82
  140.4 1.1 fusion.35
  141.5 246.2 %psum.14 = f32[16,256]{0,1:T(8,128)S(1)} all-reduce(f32[16,256]{0,1:T(8,128)S(1)} %fusion.35), channel_id=1, replica_groups=mesh['band'=64,'mem'=8] {'band'}, use_global_device_ids=true, to_apply=%region_3.4 | all-reduce | flops 4096 | bytes 32768 | tf_op jit(solution)/shard_map/psum | solution.py:94
  387.7 0.1 reshape.306
  387.8 0.1 copy.50
  387.9 16.2 %psum.15 = f32[8,4]{0,1:T(4,128)S(1)} all-reduce(f32[8,4]{0,1:T(4,128)S(1)} %reduce_sum.9), channel_id=1, replica_groups=mesh['band'=64,'mem'=8] {'mem'}, use_global_device_ids=true, to_apply=%region_5.6 | all-reduce | flops 32 | bytes 256 | tf_op jit(solution)/shard_map/psum | solution.py:99
  404.1 0.1 copy.51
  404.1 0.2 copy.48
  404.4 0.3 reshape.303
  404.6 0.8 multiply_convert_fusion.3
  405.5 0.6 broadcast_subtract_fusion
  (44 shorter events, 0.3 us)
Async XLA Ops:
  0.6 139.7 %copy-start = (bf16[2,2560,256]{2,1,0:T(8,128)(2,1)S(1)}, bf16[2,2560,256]{2,1,0:T(8,128)(2,1)}, u32[]{:S(2)}) copy-start(bf16[2,2560,256]{2,1,0:T(8,128)(2,1)} %param.11) | copy-start | bytes 7864324
  9.3 1.8 copy-start.1
  25.0 22.1 %copy-start.4 = (s32[10]{0:T(128)S(1)}, s32[10]{0:T(128)}, u32[]{:S(2)}) copy-start(s32[10]{0:T(128)} %param.9) | copy-start | bytes 124
  25.1 43.6 %copy-start.3 = (s32[64]{0:T(128)S(1)}, s32[64]{0:T(128)}, u32[]{:S(2)}) copy-start(s32[64]{0:T(128)} %param.10) | copy-start | bytes 772
  31.3 38.7 %all-to-all-start = ((bf16[64,2,640]{2,1,0:T(2,128)(2,1)}), bf16[64,2,640]{2,1,0:T(2,128)(2,1)S(1)}, u32[]{:S(2)}, u32[]{:S(2)}) async-start(bf16[64,2,640]{2,1,0:T(2,128)(2,1)} %broadcast_select_fusion), calls=%async_computation | async-start | bytes 327680 | tf_op jit(solution)/shard_map/all_to_all | solution.py:62
  71.1 13.2 %copy-start.2 = (bf16[64,2,10,2,2,4,2,2]{0,5,2,3,7,6,4,1:T(4,128)(2,1)S(1)}, bf16[64,2,10,2,2,4,2,2]{0,5,2,3,7,6,4,1:T(4,128)(2,1)}, u32[]{:S(2)}) copy-start(bf16[64,2,10,2,2,4,2,2]{0,5,2,3,7,6,4,1:T(4,128)(2,1)} %get-tuple-element.161) | copy-start | bytes 491524 | tf_op jit(solution)/shard_map/while
  84.9 13.2 %copy-start.2 = (bf16[64,2,10,2,2,4,2,2]{0,5,2,3,7,6,4,1:T(4,128)(2,1)S(1)}, bf16[64,2,10,2,2,4,2,2]{0,5,2,3,7,6,4,1:T(4,128)(2,1)}, u32[]{:S(2)}) copy-start(bf16[64,2,10,2,2,4,2,2]{0,5,2,3,7,6,4,1:T(4,128)(2,1)} %get-tuple-element.161) | copy-start | bytes 491524 | tf_op jit(solution)/shard_map/while
  98.6 13.2 %copy-start.2 = (bf16[64,2,10,2,2,4,2,2]{0,5,2,3,7,6,4,1:T(4,128)(2,1)S(1)}, bf16[64,2,10,2,2,4,2,2]{0,5,2,3,7,6,4,1:T(4,128)(2,1)}, u32[]{:S(2)}) copy-start(bf16[64,2,10,2,2,4,2,2]{0,5,2,3,7,6,4,1:T(4,128)(2,1)} %get-tuple-element.161) | copy-start | bytes 491524 | tf_op jit(solution)/shard_map/while
  112.4 13.2 %copy-start.2 = (bf16[64,2,10,2,2,4,2,2]{0,5,2,3,7,6,4,1:T(4,128)(2,1)S(1)}, bf16[64,2,10,2,2,4,2,2]{0,5,2,3,7,6,4,1:T(4,128)(2,1)}, u32[]{:S(2)}) copy-start(bf16[64,2,10,2,2,4,2,2]{0,5,2,3,7,6,4,1:T(4,128)(2,1)} %get-tuple-element.161) | copy-start | bytes 491524 | tf_op jit(solution)/shard_map/while
  126.2 13.2 %copy-start.2 = (bf16[64,2,10,2,2,4,2,2]{0,5,2,3,7,6,4,1:T(4,128)(2,1)S(1)}, bf16[64,2,10,2,2,4,2,2]{0,5,2,3,7,6,4,1:T(4,128)(2,1)}, u32[]{:S(2)}) copy-start(bf16[64,2,10,2,2,4,2,2]{0,5,2,3,7,6,4,1:T(4,128)(2,1)} %get-tuple-element.161) | copy-start | bytes 491524 | tf_op jit(solution)/shard_map/while
where the time goes:
time: 407 us; the launch traced here: 406 us
  blocking collectives  283 us (70%)
  other arithmetic  68.9 us (17%)
  local copies, waits for them, and re-layouts  23.8 us (6%)
  starting transfers between devices  13.8 us (3%)
  matrix products  11.2 us (3%)
    psum x1, blocking collectives, shards(): summed_all = lax.psum(partial_value, 'band')  246 us
    another operation x7, other arithmetic  59.7 us
    unnamed x1, blocking collectives  20.9 us
    psum x1, blocking collectives, shards(): summed = lax.psum(jnp.sum(local_share, axis=0), 'mem')  16.2 us
    all_to_all x1, starting transfers between devices, shards(): lax.all_to_all(packed, 'band', split_axis=0, concat_axis=0, tiled=True)  13.8 us
  transfers between devices with their start and end apart: 1, of which 0 were waited for; matrix products, arithmetic and copies ran while one was open for 1% of the time, Pallas kernels for 0%

commit v1 on v0

--- a/solution.py
+++ b/solution.py
@@ -91,7 +91,7 @@
         preferred_element_type=jnp.float32,
     )
     share_width = eof_modes // band_count
-    summed_all = lax.psum(partial_value, "band")
+    summed_all = jnp.sum(lax.all_gather(partial_value, "band"), axis=0)
     own_share = lax.dynamic_slice_in_dim(
         summed_all, lax.axis_index("band") * share_width, share_width, 1
     )

time: 407 us -> 253 us (0.62)
  the two profiles are of different devices: /device:TPU:8 before, /device:TPU:2 now
where the time goes in v1:
time: 253 us; the launch traced here: 252 us
  waiting for transfers between devices  78.2 us (31%)
  other arithmetic  70.3 us (28%)
  blocking collectives  36.5 us (14%)
  local copies, waits for them, and re-layouts  23.6 us (9%)
  between operations  14.9 us (6%)
  starting transfers between devices  13.9 us (5%)
  matrix products  11.1 us (4%)
  loops' own time  3.53 us (1%)
    all_gather x1, waiting for transfers between devices, shards(): summed_all = jnp.sum(lax.all_gather(partial_value, 'band'), axis=0)  78.2 us
    another operation x7, other arithmetic  59.7 us
    unnamed x1, blocking collectives  19.6 us
    psum x1, blocking collectives, shards(): summed = lax.psum(jnp.sum(local_share, axis=0), 'mem')  17 us
    all_to_all x1, starting transfers between devices, shards(): lax.all_to_all(packed, 'band', split_axis=0, concat_axis=0, tiled=True)  13.9 us
  transfers between devices with their start and end apart: 2, of which 1 were waited for; matrix products, arithmetic and copies ran while one was open for 2% of the time, Pallas kernels for 0%

profile of v1, /device:TPU:2, one launch (start us, length us, event | category | flops | bytes accessed | tf_op | source)
XLA Modules:
  0.0 252.2 jit_solution(6456985666413343002)
XLA Ops:
  7.2 0.8 broadcast_subtract_fusion.2
  8.0 0.1 broadcast_subtract_fusion.1
  8.1 0.1 compare_convert_fusion
  8.2 0.7 copy.36
  8.9 0.1 reduce-window.9
  9.0 0.1 reduce
  9.1 0.7 sub.62
  9.8 2.6 %reshape.297 = bf16[32,10,11,128]{3,2,1,0:T(8,128)(2,1)} reshape(bf16[2,4,2,2,14080]{4,3,2,1,0:T(2,128)(2,1)} %param.7) | data formatting | bytes 1802240 | tf_op jit(solution)/shard_map/reshape | solution.py:29
  12.4 3.4 %reshape.301 = bf16[40,10,11,128]{3,2,1,0:T(8,128)(2,1)} reshape(bf16[40,14080]{1,0:T(8,128)(2,1)} %param.8) | data formatting | bytes 2252800 | tf_op jit(solution)/shard_map/reshape | solution.py:30
  15.8 0.1 fusion.26
  15.9 1.5 broadcast_multiply_fusion.1
  17.4 0.2 copy-done.1
  17.6 0.1 broadcast_multiply_fusion
  17.8 2.0 fusion.20
  19.8 2.0 fusion.18
  21.8 4.0 %rev.3 = f32[10,11,32,40]{3,2,1,0:T(8,128)} reverse(f32[10,11,32,40]{3,2,1,0:T(8,128)} %fusion.18), dimensions={3} | reverse | bytes 1126400 | tf_op jit(solution)/shard_map/rev | solution.py:52
  25.7 2.6 %pad_maximum_fusion = f32[10,11,32,80]{3,2,1,0:T(8,128)S(1)} fusion(f32[10,11,32,40]{3,2,1,0:T(8,128)} %rev.3, f32[10,11,32,40]{3,2,1,0:T(8,128)} %fusion.20), kind=kLoop, calls=%fused_computation.20 | loop fusion | flops 281600 | bytes 2252800 | tf_op jit(solution)/shard_map/concatenate | solution.py:52
  28.3 3.3 %fusion.15 = bf16[80,10,2,32]{0,2,3,1:T(2,128)(2,1)S(1)} fusion(f32[10,11,32,80]{3,2,1,0:T(8,128)S(1)} %pad_maximum_fusion, f32[10,1,11]{2,1,0:T(1,128)S(1)} %broadcast_subtract_fusion.1, f32[10,1,11]{2,1,0:T(1,128)S(1)} %compare_convert_fusion), kind=kOutput, calls=%fused_computation.22 | convolution fusion | flops 6809820 | bytes 1229680 | tf_op jit(solution)/shard_map/pht,ptcj->jphc/dot_general | solution.py:53
  31.6 0.4 copy.44
  32.0 0.1 copy.43
  32.1 0.1 min.22
  32.3 2.7 %gather_fusion = bf16[128,10,2,32]{3,2,1,0:T(2,128)(2,1)} fusion(bf16[80,10,2,32]{3,2,1,0:T(2,128)(2,1)S(1)} %copy.44, s32[1024]{0:T(1024)S(1)} %pad_clamp_fusion), kind=kCustom, calls=%fused_computation | custom fusion | bytes 328192 | tf_op jit(solution)/shard_map/jit(_take)/gather | solution.py:59
  35.0 1.8 gather.7
  36.8 0.1 copy.37
  36.9 0.9 broadcast_select_fusion
  37.8 13.9 %all-to-all-start = ((bf16[64,2,640]{2,1,0:T(2,128)(2,1)}), bf16[64,2,640]{2,1,0:T(2,128)(2,1)S(1)}, u32[]{:S(2)}, u32[]{:S(2)}) async-start(bf16[64,2,640]{2,1,0:T(2,128)(2,1)} %broadcast_select_fusion), calls=%async_computation | async-start | bytes 327680 | tf_op jit(solution)/shard_map/all_to_all | solution.py:62
  51.7 1.3 dynamic-slice
  53.7 0.2 dynamic-update-slice
  53.9 19.6 %all-reduce = s32[640]{0:T(1024)S(1)} all-reduce(s32[640]{0:T(1024)S(1)} %dynamic-update-slice), channel_id=1, replica_groups=mesh['band'=64,'mem'=8] {'band'}, use_global_device_ids=true, to_apply=%add | all-reduce | flops 640 | bytes 5120
  73.5 0.1 reshape.294
  73.8 0.7 dynamic_slice.13
  74.5 0.7 compare_convert_fusion.1
  75.2 0.3 copy.45
  75.5 0.8 copy.47
  76.3 68.8 %while.12 = (s32[]{:T(128)}, f32[5,2,4,2,2,512]{5,2,3,1,4,0:T(4,128)S(1)}, s32[10,2,64]{2,0,1:T(8,128)S(1)}, s32[5]{0:T(128)S(1)}, bf16[64,2,10,2,2,4,2,2]{0,5,2,3,7,6,4,1:T(4,128)(2,1)}, /*index=5*/s32[]{:T(128)}, s32[1]{0:T(128)}) while((s32[]{:T(128)}, f32[5,2,4,2,2,512]{5,2,3,1,4,0:T(4,128)S(1)}, s32[10,2,64]{2,0,1:T(8,128)S(1)}, ...), condition=%wide.region_2.3_spmd, body=%wide.region_1.2_spmd.sunk | while | flops 97652992 | bytes 6326409 | solution.py:80
  76.3 0.6 dynamic_slice.18
  77.6 11.9 %multiply_convert_fusion.5 = (bf16[1,10,2,64,512]{4,3,1,2,0:T(8,128)(2,1)S(1)}, bf16[1,10,2,64,512]{4,3,1,2,0:T(8,128)(2,1)S(1)}) fusion(s32[512]{0:T(512)S(1)} %iota_add_fusion.2, s32[10,2,64]{2,0,1:T(8,128)S(1)} %get-tuple-element.161, f32[10,2,64]{2,0,1:T(8,128)S(1)} %get-tuple-element.141, f32[10,2,64]{2,0,1:T(8,128)S(1)} %get-tuple-element.142), kind=kLoop, calls=%fused_computation.6.clone.1 | loop fusion | flops 8519680 | bytes 2638848 | tf_op jit(solution)/shard_map/convert
  89.5 0.6 fusion.42
  90.1 0.6 dynamic_slice.18
  91.4 11.9 %multiply_convert_fusion.5 = (bf16[1,10,2,64,512]{4,3,1,2,0:T(8,128)(2,1)S(1)}, bf16[1,10,2,64,512]{4,3,1,2,0:T(8,128)(2,1)S(1)}) fusion(s32[512]{0:T(512)S(1)} %iota_add_fusion.2, s32[10,2,64]{2,0,1:T(8,128)S(1)} %get-tuple-element.161, f32[10,2,64]{2,0,1:T(8,128)S(1)} %get-tuple-element.141, f32[10,2,64]{2,0,1:T(8,128)S(1)} %get-tuple-element.142), kind=kLoop, calls=%fused_computation.6.clone.1 | loop fusion | flops 8519680 | bytes 2638848 | tf_op jit(solution)/shard_map/convert
  103.3 0.6 fusion.42
  103.8 0.6 dynamic_slice.18
  105.1 11.9 %multiply_convert_fusion.5 = (bf16[1,10,2,64,512]{4,3,1,2,0:T(8,128)(2,1)S(1)}, bf16[1,10,2,64,512]{4,3,1,2,0:T(8,128)(2,1)S(1)}) fusion(s32[512]{0:T(512)S(1)} %iota_add_fusion.2, s32[10,2,64]{2,0,1:T(8,128)S(1)} %get-tuple-element.161, f32[10,2,64]{2,0,1:T(8,128)S(1)} %get-tuple-element.141, f32[10,2,64]{2,0,1:T(8,128)S(1)} %get-tuple-element.142), kind=kLoop, calls=%fused_computation.6.clone.1 | loop fusion | flops 8519680 | bytes 2638848 | tf_op jit(solution)/shard_map/convert
  117.0 0.6 fusion.42
  117.6 0.6 dynamic_slice.18
  118.9 11.9 %multiply_convert_fusion.5 = (bf16[1,10,2,64,512]{4,3,1,2,0:T(8,128)(2,1)S(1)}, bf16[1,10,2,64,512]{4,3,1,2,0:T(8,128)(2,1)S(1)}) fusion(s32[512]{0:T(512)S(1)} %iota_add_fusion.2, s32[10,2,64]{2,0,1:T(8,128)S(1)} %get-tuple-element.161, f32[10,2,64]{2,0,1:T(8,128)S(1)} %get-tuple-element.141, f32[10,2,64]{2,0,1:T(8,128)S(1)} %get-tuple-element.142), kind=kLoop, calls=%fused_computation.6.clone.1 | loop fusion | flops 8519680 | bytes 2638848 | tf_op jit(solution)/shard_map/convert
  130.8 0.6 fusion.42
  131.4 0.6 dynamic_slice.18
  132.6 11.9 %multiply_convert_fusion.5 = (bf16[1,10,2,64,512]{4,3,1,2,0:T(8,128)(2,1)S(1)}, bf16[1,10,2,64,512]{4,3,1,2,0:T(8,128)(2,1)S(1)}) fusion(s32[512]{0:T(512)S(1)} %iota_add_fusion.2, s32[10,2,64]{2,0,1:T(8,128)S(1)} %get-tuple-element.161, f32[10,2,64]{2,0,1:T(8,128)S(1)} %get-tuple-element.141, f32[10,2,64]{2,0,1:T(8,128)S(1)} %get-tuple-element.142), kind=kLoop, calls=%fused_computation.6.clone.1 | loop fusion | flops 8519680 | bytes 2638848 | tf_op jit(solution)/shard_map/convert
  144.5 0.6 fusion.42
  145.1 0.1 multiply_convert_fusion.2
  145.2 0.1 copy.49
  145.4 0.2 convert_element_type.82
  145.6 1.1 fusion.35
  146.7 0.2 copy.48
  146.9 0.3 reshape.303
  147.1 0.8 multiply_convert_fusion.3
  148.0 78.2 %all-gather.3.cloned.1.call-done = f32[1024,256]{1,0:T(8,128)} async-done(((f32[16,256]{1,0:T(8,128)}), f32[1024,256]{1,0:T(8,128)}) %all-gather.3.cloned.1.call-update) | async-done | bytes 1048592 | tf_op jit(solution)/shard_map/all_gather | solution.py:94
  226.2 1.3 reduce_sum.18
  227.5 0.1 bitcast_reduce_fusion
  227.6 0.1 copy.56
  227.7 17.0 %psum.7 = f32[8,4]{0,1:T(4,128)S(1)} all-reduce(f32[8,4]{0,1:T(4,128)S(1)} %copy.56), channel_id=1, replica_groups=mesh['band'=64,'mem'=8] {'mem'}, use_global_device_ids=true, to_apply=%region_5.6 | all-reduce | flops 32 | bytes 256 | tf_op jit(solution)/shard_map/psum | solution.py:99
  244.6 0.1 copy.51
  244.7 0.6 broadcast_subtract_fusion
  (45 shorter events, 0.4 us)
Async XLA Ops:
  7.2 138.4 %copy-start = (bf16[2,2560,256]{2,1,0:T(8,128)(2,1)S(1)}, bf16[2,2560,256]{2,1,0:T(8,128)(2,1)}, u32[]{:S(2)}) copy-start(bf16[2,2560,256]{2,1,0:T(8,128)(2,1)} %param.11) | copy-start | bytes 7864324
  15.8 1.8 copy-start.1
  31.6 22.1 %copy-start.4 = (s32[10]{0:T(128)S(1)}, s32[10]{0:T(128)}, u32[]{:S(2)}) copy-start(s32[10]{0:T(128)} %param.9) | copy-start | bytes 124
  31.6 42.2 %copy-start.3 = (s32[64]{0:T(128)S(1)}, s32[64]{0:T(128)}, u32[]{:S(2)}) copy-start(s32[64]{0:T(128)} %param.10) | copy-start | bytes 772
  37.8 37.4 %all-to-all-start = ((bf16[64,2,640]{2,1,0:T(2,128)(2,1)}), bf16[64,2,640]{2,1,0:T(2,128)(2,1)S(1)}, u32[]{:S(2)}, u32[]{:S(2)}) async-start(bf16[64,2,640]{2,1,0:T(2,128)(2,1)} %broadcast_select_fusion), calls=%async_computation | async-start | bytes 327680 | tf_op jit(solution)/shard_map/all_to_all | solution.py:62
  51.7 174.5 %all-gather.3.cloned.1.call-start = ((), (), s32[]{:S(2)}) async-start(), calls=%async_computation.1 | async-start | bytes 1064960 | tf_op jit(solution)/shard_map/all_gather | solution.py:94
  76.3 13.2 %copy-start.2 = (bf16[64,2,10,2,2,4,2,2]{0,5,2,3,7,6,4,1:T(4,128)(2,1)S(1)}, bf16[64,2,10,2,2,4,2,2]{0,5,2,3,7,6,4,1:T(4,128)(2,1)}, u32[]{:S(2)}) copy-start(bf16[64,2,10,2,2,4,2,2]{0,5,2,3,7,6,4,1:T(4,128)(2,1)} %get-tuple-element.163) | copy-start | bytes 491524 | tf_op jit(solution)/shard_map/while
  90.1 13.2 %copy-start.2 = (bf16[64,2,10,2,2,4,2,2]{0,5,2,3,7,6,4,1:T(4,128)(2,1)S(1)}, bf16[64,2,10,2,2,4,2,2]{0,5,2,3,7,6,4,1:T(4,128)(2,1)}, u32[]{:S(2)}) copy-start(bf16[64,2,10,2,2,4,2,2]{0,5,2,3,7,6,4,1:T(4,128)(2,1)} %get-tuple-element.163) | copy-start | bytes 491524 | tf_op jit(solution)/shard_map/while
  103.8 13.2 %copy-start.2 = (bf16[64,2,10,2,2,4,2,2]{0,5,2,3,7,6,4,1:T(4,128)(2,1)S(1)}, bf16[64,2,10,2,2,4,2,2]{0,5,2,3,7,6,4,1:T(4,128)(2,1)}, u32[]{:S(2)}) copy-start(bf16[64,2,10,2,2,4,2,2]{0,5,2,3,7,6,4,1:T(4,128)(2,1)} %get-tuple-element.163) | copy-start | bytes 491524 | tf_op jit(solution)/shard_map/while
  117.6 13.2 %copy-start.2 = (bf16[64,2,10,2,2,4,2,2]{0,5,2,3,7,6,4,1:T(4,128)(2,1)S(1)}, bf16[64,2,10,2,2,4,2,2]{0,5,2,3,7,6,4,1:T(4,128)(2,1)}, u32[]{:S(2)}) copy-start(bf16[64,2,10,2,2,4,2,2]{0,5,2,3,7,6,4,1:T(4,128)(2,1)} %get-tuple-element.163) | copy-start | bytes 491524 | tf_op jit(solution)/shard_map/while
  131.4 13.2 %copy-start.2 = (bf16[64,2,10,2,2,4,2,2]{0,5,2,3,7,6,4,1:T(4,128)(2,1)S(1)}, bf16[64,2,10,2,2,4,2,2]{0,5,2,3,7,6,4,1:T(4,128)(2,1)}, u32[]{:S(2)}) copy-start(bf16[64,2,10,2,2,4,2,2]{0,5,2,3,7,6,4,1:T(4,128)(2,1)} %get-tuple-element.163) | copy-start | bytes 491524 | tf_op jit(solution)/shard_map/while
Sparse Core Ops, SparseCore 0:
  146.8 79.3 all-gather.2
